TPU v7x, 32 devices: a whole 2x2x4 slice. The times are simulated.
32 devices in a mesh: dp: 8 (over y, x, core), seq: 4 (over z).
Axes of the slice: x: 2, y: 2, z: 4, core: 2. Of those that a mesh axis runs over, the one named last changes fastest.
Arguments:
- inputs: bfloat16 [24, 1024, 768], P('dp', 'seq'), may hold values from -6 to 6
- segment_ids: int32 [24, 1024], P('dp', 'seq'), may hold values from 0 to 3, never falling along the last dimension, each value on 1 to 512 neighbouring positions
- norm1_gain: bfloat16 [768], P('dp'), may hold values from 0.5 to 1.5
- norm1_shift: bfloat16 [768], P('dp'), may hold values from -1.5 to 1.5
- query_weight: bfloat16 [768, 768], P('dp'), may hold values from -0.4375 to 0.4375
- query_bias: bfloat16 [768], P('dp'), may hold values from -2.5 to 2.5
- key_weight: bfloat16 [768, 768], P('dp'), may hold values from -0.21875 to 0.21875
- value_weight: bfloat16 [768, 768], P('dp'), may hold values from -0.21875 to 0.21875
- value_bias: bfloat16 [768], P('dp'), may hold values from -1.5 to 1.5
- out_weight: bfloat16 [768, 768], P('dp'), may hold values from -0.625 to 0.625
- out_bias: bfloat16 [768], P('dp'), may hold values from -1.5 to 1.5
- norm2_gain: bfloat16 [768], P('dp'), may hold values from 0.5 to 1.5
- norm2_shift: bfloat16 [768], P('dp'), may hold values from -1.5 to 1.5
- fc1_weight: bfloat16 [768, 3072], P('dp'), may hold values from -0.21875 to 0.21875
- fc1_bias: bfloat16 [3072], P('dp'), may hold values from -1.5 to 1.5
- fc2_weight: bfloat16 [3072, 768], P('dp'), may hold values from -0.15625 to 0.15625
- fc2_bias: bfloat16 [768], P('dp'), may hold values from -1.5 to 1.5
- grad_output: bfloat16 [24, 1024, 768], P('dp', 'seq'), may hold values from -6 to 6
Outputs:
- output: bfloat16 [24, 1024, 768], P('dp', 'seq')
- grad_inputs: bfloat16 [24, 1024, 768], P('dp', 'seq')
- grad_norm1_gain: float32 [768], P('dp')
- grad_norm1_shift: float32 [768], P('dp')
- grad_query_weight: float32 [768, 768], P('dp')
- grad_query_bias: float32 [768], P('dp')
- grad_key_weight: float32 [768, 768], P('dp')
- grad_value_weight: float32 [768, 768], P('dp')
- grad_value_bias: float32 [768], P('dp')
- grad_out_weight: float32 [768, 768], P('dp')
- grad_out_bias: float32 [768], P('dp')
- grad_norm2_gain: float32 [768], P('dp')
- grad_norm2_shift: float32 [768], P('dp')
- grad_fc1_weight: float32 [768, 3072], P('dp')
- grad_fc1_bias: float32 [3072], P('dp')
- grad_fc2_weight: float32 [3072, 768], P('dp')
- grad_fc2_bias: float32 [768], P('dp')
Inputs may be any that keep to these rules, and one draw needn't show every extreme that they name: `segment_ids`: within each sequence, segment numbers never fall along the positions; each segment is a run of 1 to 512 positions.
All inputs are finite; a program needn't handle non-finite values.
Results may differ from a plain program's by a relative error of at most 0.017.
Values may be sent and summed in bfloat16 or wider, within the bound.
No kernel may reach another device: no remote copies, remote signals or barrier semaphores. Data moves between devices by JAX's collectives and lax.ppermute only.
A program may use at most 192 MiB of HBM per device.

v0:
```python
import jax
import jax.numpy as jnp
from jax import lax
from jax.sharding import PartitionSpec as P

HD = 64
EPSILON = 1e-05


def layer_norm(values, gain, shift):
    center = values - jnp.mean(values, axis=-1, keepdims=True)
    inverse = lax.rsqrt(jnp.mean(center * center, axis=-1, keepdims=True) + EPSILON)
    normed = center * inverse
    return (normed * gain + shift, normed, inverse)


def norm_back(grad, normed, inverse, gain):
    scaled = grad * gain
    return inverse * (
        scaled
        - jnp.mean(scaled, axis=-1, keepdims=True)
        - normed * jnp.mean(scaled * normed, axis=-1, keepdims=True)
    )


def gelu_slope(pre_act):
    return (
        0.5 * (1.0 + lax.erf(pre_act * 0.7071067811865476))
        + pre_act * jnp.exp(-0.5 * pre_act * pre_act) * 0.3989422804014327
    )


def cross_rows(left, right):
    return lax.dot_general(
        left, right, (((0,), (0,)), ((), ())), preferred_element_type=jnp.float32
    )


def times_transpose(left, right):
    return lax.dot_general(
        left, right, (((1,), (1,)), ((), ())), preferred_element_type=jnp.float32
    )


def to_pairs(array, heads_here):
    seqs_here, positions, _ = array.shape
    shaped = array.reshape(seqs_here, positions, heads_here, HD).transpose(0, 2, 1, 3)
    return shaped.reshape(seqs_here * heads_here, positions, HD)


def from_pairs(array, seqs_here, heads_here):
    positions = array.shape[1]
    shaped = array.reshape(seqs_here, heads_here, positions, HD).transpose(0, 2, 1, 3)
    return shaped.reshape(seqs_here, positions, heads_here * HD)


def masked_scores(query_pair, key_pair, segment_row):
    scores = jnp.einsum(
        "qd,kd->qk", query_pair, key_pair, preferred_element_type=jnp.float32
    ) * HD ** (-0.5)
    same_segment = segment_row[:, None] == segment_row[None, :]
    return jnp.where(same_segment, scores, -1e30)


def attend_forward(packed):
    query_pair, key_pair, value_pair, segment_row = packed
    scores = masked_scores(query_pair, key_pair, segment_row)
    highest = jnp.max(scores, axis=-1, keepdims=True)
    expon = jnp.exp(scores - highest)
    totals = jnp.sum(expon, axis=-1, keepdims=True)
    probs = (expon / totals).astype(jnp.bfloat16)
    result = jnp.dot(probs, value_pair, preferred_element_type=jnp.float32).astype(jnp.bfloat16)
    return (result, (highest + jnp.log(totals))[:, 0])


def attend_backward(packed):
    query_pair, key_pair, value_pair, segment_row, logsum, grad_pair = packed
    scores = masked_scores(query_pair, key_pair, segment_row)
    probs = jnp.exp(scores - logsum[:, None])
    grad_probs = jnp.einsum("qd,kd->qk", grad_pair, value_pair, preferred_element_type=jnp.float32)
    delta = jnp.sum(probs * grad_probs, axis=-1, keepdims=True)
    grad_scores = (probs * (grad_probs - delta)).astype(jnp.bfloat16)
    factor = HD ** (-0.5)
    grad_query = (
        jnp.einsum("qk,kd->qd", grad_scores, key_pair, preferred_element_type=jnp.float32) * factor
    ).astype(jnp.bfloat16)
    grad_key = (
        jnp.einsum("qk,qd->kd", grad_scores, query_pair, preferred_element_type=jnp.float32)
        * factor
    ).astype(jnp.bfloat16)
    grad_value = jnp.einsum(
        "qk,qd->kd", probs.astype(jnp.bfloat16), grad_pair, preferred_element_type=jnp.float32
    ).astype(jnp.bfloat16)
    return (grad_query, grad_key, grad_value)


def column_sum(array):
    return jnp.sum(array.astype(jnp.float32), axis=0)


def per_device(
    inputs,
    segment_ids,
    norm1_gain,
    norm1_shift,
    query_weight,
    query_bias,
    key_weight,
    value_weight,
    value_bias,
    out_weight,
    out_bias,
    norm2_gain,
    norm2_shift,
    fc1_weight,
    fc1_bias,
    fc2_weight,
    fc2_bias,
    grad_output,
):
    seqs_here, positions, model_width = inputs.shape
    token_rows = seqs_here * positions
    (
        first_gain,
        first_shift,
        w_query,
        b_query,
        w_key,
        w_value,
        b_value,
        w_out,
        b_out,
        second_gain,
        second_shift,
        w_up,
        b_up,
        w_down,
        b_down,
    ) = (
        lax.all_gather(norm1_gain, "dp", axis=0, tiled=True),
        lax.all_gather(norm1_shift, "dp", axis=0, tiled=True),
        lax.all_gather(query_weight, "dp", axis=0, tiled=True),
        lax.all_gather(query_bias, "dp", axis=0, tiled=True),
        lax.all_gather(key_weight, "dp", axis=0, tiled=True),
        lax.all_gather(value_weight, "dp", axis=0, tiled=True),
        lax.all_gather(value_bias, "dp", axis=0, tiled=True),
        lax.all_gather(out_weight, "dp", axis=0, tiled=True),
        lax.all_gather(out_bias, "dp", axis=0, tiled=True),
        lax.all_gather(norm2_gain, "dp", axis=0, tiled=True),
        lax.all_gather(norm2_shift, "dp", axis=0, tiled=True),
        lax.all_gather(fc1_weight, "dp", axis=0, tiled=True),
        lax.all_gather(fc1_bias, "dp", axis=0, tiled=True),
        lax.all_gather(fc2_weight, "dp", axis=0, tiled=True),
        lax.all_gather(fc2_bias, "dp", axis=0, tiled=True),
    )
    full_segments = lax.all_gather(segment_ids, "seq", axis=1, tiled=True)
    flat_in = inputs.reshape(token_rows, model_width).astype(jnp.float32)
    normed_one, unit_one, inverse_one = layer_norm(
        flat_in, first_gain.astype(jnp.float32), first_shift.astype(jnp.float32)
    )
    act_one = normed_one.astype(jnp.bfloat16)
    query_tok = (
        jnp.dot(act_one, w_query, preferred_element_type=jnp.float32) + b_query.astype(jnp.float32)
    ).astype(jnp.bfloat16)
    key_tok = jnp.dot(act_one, w_key, preferred_element_type=jnp.float32).astype(jnp.bfloat16)
    value_tok = (
        jnp.dot(act_one, w_value, preferred_element_type=jnp.float32) + b_value.astype(jnp.float32)
    ).astype(jnp.bfloat16)
    query_heads, key_heads, value_heads = (
        lax.all_to_all(
            query_tok.reshape(seqs_here, positions, model_width),
            "seq",
            split_axis=2,
            concat_axis=1,
            tiled=True,
        ),
        lax.all_to_all(
            key_tok.reshape(seqs_here, positions, model_width),
            "seq",
            split_axis=2,
            concat_axis=1,
            tiled=True,
        ),
        lax.all_to_all(
            value_tok.reshape(seqs_here, positions, model_width),
            "seq",
            split_axis=2,
            concat_axis=1,
            tiled=True,
        ),
    )
    heads_here = query_heads.shape[2] // HD
    query_pairs = to_pairs(query_heads, heads_here)
    key_pairs = to_pairs(key_heads, heads_here)
    value_pairs = to_pairs(value_heads, heads_here)
    segment_pairs = jnp.repeat(full_segments, heads_here, axis=0)
    attn_pairs, logsum = lax.map(
        attend_forward, (query_pairs, key_pairs, value_pairs, segment_pairs)
    )
    attn_heads = from_pairs(attn_pairs, seqs_here, heads_here)
    attn_tok = lax.all_to_all(attn_heads, "seq", split_axis=1, concat_axis=2, tiled=True).reshape(
        token_rows, model_width
    )
    middle = (
        flat_in
        + jnp.dot(attn_tok, w_out, preferred_element_type=jnp.float32)
        + b_out.astype(jnp.float32)
    )
    normed_two, unit_two, inverse_two = layer_norm(
        middle, second_gain.astype(jnp.float32), second_shift.astype(jnp.float32)
    )
    act_two = normed_two.astype(jnp.bfloat16)
    pre_act = jnp.dot(act_two, w_up, preferred_element_type=jnp.float32) + b_up.astype(jnp.float32)
    hidden = jax.nn.gelu(pre_act, approximate=False).astype(jnp.bfloat16)
    result = (
        middle
        + jnp.dot(hidden, w_down, preferred_element_type=jnp.float32)
        + b_down.astype(jnp.float32)
    )
    output = result.astype(jnp.bfloat16).reshape(seqs_here, positions, model_width)
    first_gain_b, w_query_b, w_key_b, w_value_b, w_out_b, second_gain_b, w_up_b, w_down_b = (
        lax.all_gather(norm1_gain, "dp", axis=0, tiled=True),
        lax.all_gather(query_weight, "dp", axis=0, tiled=True),
        lax.all_gather(key_weight, "dp", axis=0, tiled=True),
        lax.all_gather(value_weight, "dp", axis=0, tiled=True),
        lax.all_gather(out_weight, "dp", axis=0, tiled=True),
        lax.all_gather(norm2_gain, "dp", axis=0, tiled=True),
        lax.all_gather(fc1_weight, "dp", axis=0, tiled=True),
        lax.all_gather(fc2_weight, "dp", axis=0, tiled=True),
    )
    grad_down = grad_output.reshape(token_rows, model_width)
    d_b_down = column_sum(grad_down)
    d_w_down = cross_rows(hidden, grad_down)
    grad_hidden = times_transpose(grad_down, w_down_b)
    grad_pre = (grad_hidden * gelu_slope(pre_act)).astype(jnp.bfloat16)
    d_b_up = column_sum(grad_pre)
    d_w_up = cross_rows(act_two, grad_pre)
    grad_two = times_transpose(grad_pre, w_up_b)
    d_second_gain = jnp.sum(grad_two * unit_two, axis=0)
    d_second_shift = jnp.sum(grad_two, axis=0)
    grad_middle = grad_down.astype(jnp.float32) + norm_back(
        grad_two, unit_two, inverse_two, second_gain_b.astype(jnp.float32)
    )
    grad_branch = grad_middle.astype(jnp.bfloat16)
    d_b_out = column_sum(grad_branch)
    d_w_out = cross_rows(attn_tok, grad_branch)
    grad_attn = (
        times_transpose(grad_branch, w_out_b)
        .astype(jnp.bfloat16)
        .reshape(seqs_here, positions, model_width)
    )
    grad_attn_heads = lax.all_to_all(grad_attn, "seq", split_axis=2, concat_axis=1, tiled=True)
    grad_query_pairs, grad_key_pairs, grad_value_pairs = lax.map(
        attend_backward,
        (
            query_pairs,
            key_pairs,
            value_pairs,
            segment_pairs,
            logsum,
            to_pairs(grad_attn_heads, heads_here),
        ),
    )
    grad_query_tok, grad_key_tok, grad_value_tok = (
        lax.all_to_all(
            from_pairs(grad_query_pairs, seqs_here, heads_here),
            "seq",
            split_axis=1,
            concat_axis=2,
            tiled=True,
        ),
        lax.all_to_all(
            from_pairs(grad_key_pairs, seqs_here, heads_here),
            "seq",
            split_axis=1,
            concat_axis=2,
            tiled=True,
        ),
        lax.all_to_all(
            from_pairs(grad_value_pairs, seqs_here, heads_here),
            "seq",
            split_axis=1,
            concat_axis=2,
            tiled=True,
        ),
    )
    grad_query_tok = grad_query_tok.reshape(token_rows, model_width)
    grad_key_tok = grad_key_tok.reshape(token_rows, model_width)
    grad_value_tok = grad_value_tok.reshape(token_rows, model_width)
    d_b_query = column_sum(grad_query_tok)
    d_b_value = column_sum(grad_value_tok)
    d_w_query = cross_rows(act_one, grad_query_tok)
    d_w_key = cross_rows(act_one, grad_key_tok)
    d_w_value = cross_rows(act_one, grad_value_tok)
    grad_one = (
        times_transpose(grad_query_tok, w_query_b)
        + times_transpose(grad_key_tok, w_key_b)
        + times_transpose(grad_value_tok, w_value_b)
    )
    d_first_gain = jnp.sum(grad_one * unit_one, axis=0)
    d_first_shift = jnp.sum(grad_one, axis=0)
    grad_inputs = grad_middle + norm_back(
        grad_one, unit_one, inverse_one, first_gain_b.astype(jnp.float32)
    )
    grad_inputs = grad_inputs.astype(jnp.bfloat16).reshape(seqs_here, positions, model_width)
    (
        part_first_gain,
        part_first_shift,
        part_w_query,
        part_b_query,
        part_w_key,
        part_w_value,
        part_b_value,
        part_w_out,
        part_b_out,
        part_second_gain,
        part_second_shift,
        part_w_up,
        part_b_up,
        part_w_down,
        part_b_down,
    ) = (
        lax.psum_scatter(d_first_gain, "dp", scatter_dimension=0, tiled=True),
        lax.psum_scatter(d_first_shift, "dp", scatter_dimension=0, tiled=True),
        lax.psum_scatter(d_w_query, "dp", scatter_dimension=0, tiled=True),
        lax.psum_scatter(d_b_query, "dp", scatter_dimension=0, tiled=True),
        lax.psum_scatter(d_w_key, "dp", scatter_dimension=0, tiled=True),
        lax.psum_scatter(d_w_value, "dp", scatter_dimension=0, tiled=True),
        lax.psum_scatter(d_b_value, "dp", scatter_dimension=0, tiled=True),
        lax.psum_scatter(d_w_out, "dp", scatter_dimension=0, tiled=True),
        lax.psum_scatter(d_b_out, "dp", scatter_dimension=0, tiled=True),
        lax.psum_scatter(d_second_gain, "dp", scatter_dimension=0, tiled=True),
        lax.psum_scatter(d_second_shift, "dp", scatter_dimension=0, tiled=True),
        lax.psum_scatter(d_w_up, "dp", scatter_dimension=0, tiled=True),
        lax.psum_scatter(d_b_up, "dp", scatter_dimension=0, tiled=True),
        lax.psum_scatter(d_w_down, "dp", scatter_dimension=0, tiled=True),
        lax.psum_scatter(d_b_down, "dp", scatter_dimension=0, tiled=True),
    )
    (
        shard_first_gain,
        shard_first_shift,
        shard_w_query,
        shard_b_query,
        shard_w_key,
        shard_w_value,
        shard_b_value,
        shard_w_out,
        shard_b_out,
        shard_second_gain,
        shard_second_shift,
        shard_w_up,
        shard_b_up,
        shard_w_down,
        shard_b_down,
    ) = (
        lax.psum(part_first_gain.astype(jnp.bfloat16), "seq").astype(jnp.float32),
        lax.psum(part_first_shift.astype(jnp.bfloat16), "seq").astype(jnp.float32),
        lax.psum(part_w_query.astype(jnp.bfloat16), "seq").astype(jnp.float32),
        lax.psum(part_b_query.astype(jnp.bfloat16), "seq").astype(jnp.float32),
        lax.psum(part_w_key.astype(jnp.bfloat16), "seq").astype(jnp.float32),
        lax.psum(part_w_value.astype(jnp.bfloat16), "seq").astype(jnp.float32),
        lax.psum(part_b_value.astype(jnp.bfloat16), "seq").astype(jnp.float32),
        lax.psum(part_w_out.astype(jnp.bfloat16), "seq").astype(jnp.float32),
        lax.psum(part_b_out.astype(jnp.bfloat16), "seq").astype(jnp.float32),
        lax.psum(part_second_gain.astype(jnp.bfloat16), "seq").astype(jnp.float32),
        lax.psum(part_second_shift.astype(jnp.bfloat16), "seq").astype(jnp.float32),
        lax.psum(part_w_up.astype(jnp.bfloat16), "seq").astype(jnp.float32),
        lax.psum(part_b_up.astype(jnp.bfloat16), "seq").astype(jnp.float32),
        lax.psum(part_w_down.astype(jnp.bfloat16), "seq").astype(jnp.float32),
        lax.psum(part_b_down.astype(jnp.bfloat16), "seq").astype(jnp.float32),
    )
    return (
        output,
        grad_inputs,
        shard_first_gain,
        shard_first_shift,
        shard_w_query,
        shard_b_query,
        shard_w_key,
        shard_w_value,
        shard_b_value,
        shard_w_out,
        shard_b_out,
        shard_second_gain,
        shard_second_shift,
        shard_w_up,
        shard_b_up,
        shard_w_down,
        shard_b_down,
    )


def solution(mesh):
    placed = (
        P("dp", "seq", None),
        P("dp", "seq"),
        P("dp"),
        P("dp"),
        P("dp", None),
        P("dp"),
        P("dp", None),
        P("dp", None),
        P("dp"),
        P("dp", None),
        P("dp"),
        P("dp"),
        P("dp"),
        P("dp", None),
        P("dp"),
        P("dp", None),
        P("dp"),
        P("dp", "seq", None),
    )
    return jax.shard_map(
        per_device,
        mesh=mesh,
        in_specs=placed,
        out_specs=(
            P("dp", "seq", None),
            P("dp", "seq", None),
            P("dp"),
            P("dp"),
            P("dp", None),
            P("dp"),
            P("dp", None),
            P("dp", None),
            P("dp"),
            P("dp", None),
            P("dp"),
            P("dp"),
            P("dp"),
            P("dp", None),
            P("dp"),
            P("dp", None),
            P("dp"),
        ),
        check_vma=False,
    )
```

profile of v0, /device:TPU:0, one launch (start us, length us, event | category | flops | bytes accessed | tf_op | source)
XLA Modules:
  0.0 1093.1 jit_solution(9284306337476619404)
XLA Ops:
  15.2 26.3 %all-reduce.18 = (bf16[768]{0:T(1024)(128)(2,1)S(1)}, bf16[768]{0:T(1024)(128)(2,1)S(1)}, bf16[768]{0:T(1024)(128)(2,1)S(1)}, bf16[768]{0:T(1024)(128)(2,1)S(1)}...) all-reduce(bf16[768]{0:T(1024)(128)(2,1)S(1)} %dynamic-update-slice, ...), channel_id=1, replica_groups=mesh['dp'=8,'seq'=4] {'dp'}, use_global_device_ids=true, to_apply=%add.1 | all-reduce | flops 6144 | bytes 24576
  47.7 5.0 all-to-all-start
  53.4 9.6 all-gather.12.cloned.1.call-done
  62.9 3.7 add_convert_fusion.2
  66.7 3.6 copy.106
  70.2 16.2 %all-to-all-done = bf16[3,256,768]{1,0,2:T(4,128)(2,1)S(1)} async-done(((bf16[3,256,768]{1,0,2:T(4,128)(2,1)}), bf16[3,256,768]{1,0,2:T(4,128)(2,1)S(1)}, u32[]{:S(2)}, u32[]{:S(2)}) %all-to-all-start) | async-done | bytes 1179680 | tf_op jit(solution)/shard_map/all_to_all | solution.py:170
  86.5 4.3 all-to-all-start.2
  91.4 3.7 convolution_convert_fusion.1
  95.1 3.6 copy.103
  98.7 28.6 %all-to-all-done.2 = bf16[3,256,768]{1,0,2:T(4,128)(2,1)} async-done(((bf16[3,256,768]{1,0,2:T(4,128)(2,1)}), bf16[3,256,768]{1,0,2:T(4,128)(2,1)}, u32[]{:S(2)}, u32[]{:S(2)}) %all-to-all-start.2) | async-done | bytes 1179680 | tf_op jit(solution)/shard_map/all_to_all | solution.py:184
  127.3 4.3 all-to-all-start.1
  132.3 41.2 %all_gather.56 = s32[3,1024]{1,0:T(4,128)S(1)} all-gather(s32[3,256]{1,0:T(4,128)S(1)} %copy-done.26), channel_id=1, replica_groups=mesh['dp'=8,'seq'=4] {'seq'}, dimensions={1}, use_global_device_ids=true | all-gather | bytes 15360 | tf_op jit(solution)/shard_map/all_gather | solution.py:156
  183.2 3.4 reshape.295
  186.6 3.7 copy.111
  197.2 3.7 copy.110
  202.1 99.2 %while.26 = (s32[]{:T(128)}, bf16[9,1024,64]{1,2,0:T(8,128)(2,1)}, f32[9,1024]{1,0:T(8,128)}, s32[9,1024]{1,0:T(8,128)}, bf16[9,1024,64]{2,1,0:T(8,128)(2,1)S(1)...) while((s32[]{:T(128)}, bf16[9,1024,64]{1,2,0:T(8,128)(2,1)}, ...), condition=%wide.region_5.6_spmd, body=%wide.region_2.5_spmd.sunk | while | flops 284228608 | bytes 30349440 | solution.py:197
  208.9 4.2 fusion.156
  219.9 4.2 fusion.156
  231.0 4.2 fusion.156
  242.0 4.2 fusion.156
  253.0 4.2 fusion.156
  264.0 4.2 fusion.156
  275.0 4.2 fusion.156
  286.0 4.2 fusion.156
  297.1 4.2 fusion.156
  301.3 4.2 copy.112
  305.5 4.6 all-to-all-start.3
  311.4 10.1 all-gather
  322.1 33.6 %all-to-all-done.3 = bf16[3,1024,192]{2,0,1:T(4,128)(2,1)} async-done(((bf16[3,1024,192]{2,0,1:T(4,128)(2,1)}), bf16[3,1024,192]{2,0,1:T(4,128)(2,1)}, u32[]{:S(2)}, u32[]{:S(2)}) %all-to-all-start.3) | async-done | bytes 1179680 | tf_op jit(solution)/shard_map/all_to_all | solution.py:201
  364.3 27.2 %fusion.56 = (bf16[768,3072]{1,0:T(8,128)(2,1)}, f32[768,3072]{1,0:T(8,128)}) fusion(f32[3072]{0:T(1024)} %bitcast.275, bf16[768,3072]{1,0:T(8,128)(2,1)} %all-gather.16.cloned.1.call-done, f32[768,768]{1,0:T(8,128)S(1)} %get-tuple-element.265, f32[768]{0:T(1024)S(1)} %convert_element_type.227, f32[768]{0:T(1024)S(1)} %convert_element_type.226, ...), kind=kOutput, calls=%fused_computation.64 | convolution fusion | flops 3782541312 | bytes 21258240 | tf_op jit(solution)/shard_map/dot_general | solution.py:213
  391.5 11.6 %convert_reduce_fusion = (f32[3072]{0:T(1024)}, bf16[768,3072]{1,0:T(8,128)(2,1)S(1)}) fusion(f32[768,3072]{1,0:T(8,128)} %get-tuple-element.267, f32[3072]{0:T(1024)} %bitcast.276, bf16[768,768]{1,0:T(8,128)(2,1)} %bitcast.249, bf16[3072,768]{1,0:T(8,128)(2,1)} %all-gather.18.cloned.1.call-done), kind=kOutput, calls=%fused_computation.71 | convolution fusion | flops 3654546432 | bytes 20078592 | tf_op jit(solution)/shard_map/dot_general | solution.py:40
  403.2 4.8 multiply_reduce_fusion.1
  411.8 3.6 copy.115
  415.4 4.3 all-to-all-start.4
  419.8 4.5 fusion.90
  424.4 31.9 %all-to-all-done.4 = bf16[3,256,768]{1,0,2:T(4,128)(2,1)} async-done(((bf16[3,256,768]{1,0,2:T(4,128)(2,1)}), bf16[3,256,768]{1,0,2:T(4,128)(2,1)}, u32[]{:S(2)}, u32[]{:S(2)}) %all-to-all-start.4) | async-done | bytes 1179680 | tf_op jit(solution)/shard_map/all_to_all | solution.py:252
  459.8 3.8 reshape.303
  467.1 124.2 %while.27 = (s32[]{:T(128)}, bf16[9,1024,64]{1,2,0:T(8,128)(2,1)}, bf16[9,1024,64]{1,2,0:T(8,128)(2,1)}, bf16[9,1024,64]{1,2,0:T(8,128)(2,1)}, s32[9,1024]{1,0:T...) while((s32[]{:T(128)}, bf16[9,1024,64]{1,2,0:T(8,128)(2,1)}, ...), condition=%wide.region_12.13_spmd, body=%wide.region_10.12_spmd.sunk | while | flops 681901056 | bytes 33465460 | solution.py:253
  591.2 4.1 copy.122
  595.3 4.4 all-to-all-start.5
  602.0 45.4 %all-to-all-done.5 = bf16[3,1024,192]{2,0,1:T(4,128)(2,1)} async-done(((bf16[3,1024,192]{2,0,1:T(4,128)(2,1)}), bf16[3,1024,192]{2,0,1:T(4,128)(2,1)}, u32[]{:S(2)}, u32[]{:S(2)}) %all-to-all-start.5) | async-done | bytes 1179680 | tf_op jit(solution)/shard_map/all_to_all | solution.py:265
  647.5 4.2 copy.124
  651.7 4.0 reshape.307
  655.7 4.2 fusion.99
  660.0 4.1 copy.125
  664.0 51.4 %all_to_all.120 = bf16[3,1024,192]{2,0,1:T(4,128)(2,1)S(1)} all-to-all(bf16[3,1024,192]{2,0,1:T(4,128)(2,1)} %copy.125), channel_id=1, replica_groups=mesh['dp'=8,'seq'=4] {'seq'}, dimensions={1} | all-to-all | bytes 2359296 | tf_op jit(solution)/shard_map/all_to_all | solution.py:272
  718.1 4.0 reshape.310
  722.1 4.2 fusion.100
  726.4 4.1 copy.128
  730.5 50.8 %all_to_all.121 = bf16[3,1024,192]{2,0,1:T(4,128)(2,1)S(1)} all-to-all(bf16[3,1024,192]{2,0,1:T(4,128)(2,1)} %copy.128), channel_id=1, replica_groups=mesh['dp'=8,'seq'=4] {'seq'}, dimensions={1} | all-to-all | bytes 2359296 | tf_op jit(solution)/shard_map/all_to_all | solution.py:279
  785.3 4.0 reshape.313
  789.3 4.1 fusion.101
  793.5 9.0 fusion.93
  802.6 10.6 fusion.102
  817.2 8.6 add_convert_fusion
  825.8 4.4 copy.135
  839.9 4.1 fusion.97
  849.0 67.9 %reduce-scatter.15.cloned.1.call-done = f32[96,3072]{1,0:T(8,128)} async-done(((f32[768,3072]{1,0:T(8,128)}), f32[96,3072]{1,0:T(8,128)}) %reduce-scatter.15.cloned.1.call-update) | async-done | bytes 1179664 | tf_op jit(solution)/shard_map/reduce_scatter | solution.py:334
  919.0 77.7 %reduce-scatter.17.cloned.1.call-done = f32[384,768]{1,0:T(8,128)} async-done(((f32[3072,768]{1,0:T(8,128)}), f32[384,768]{1,0:T(8,128)}) %reduce-scatter.17.cloned.1.call-update) | async-done | bytes 1179664 | tf_op jit(solution)/shard_map/reduce_scatter | solution.py:336
  1001.3 3.8 fusion.88
  1005.2 26.3 %all-reduce.17 = (bf16[768]{0:T(1024)(128)(2,1)}, bf16[768]{0:T(1024)(128)(2,1)}, bf16[768]{0:T(1024)(128)(2,1)}, bf16[768]{0:T(1024)(128)(2,1)}, bf16[768]{0:T(...) all-reduce(f32[768]{0:T(1024)} %get-tuple-element.184, ...), channel_id=2, replica_groups=mesh['dp'=8,'seq'=4] {'dp'}, use_global_device_ids=true, to_apply=%region_16.17.clone | all-reduce | flops 9216 | bytes 55296
  1042.2 13.1 %all-reduce.19 = (bf16[96]{0:T(256)(128)(2,1)}, bf16[96]{0:T(256)(128)(2,1)}, bf16[96]{0:T(256)(128)(2,1)}, bf16[96]{0:T(256)(128)(2,1)}, bf16[96]{0:T(256)(128)...) all-reduce(bf16[96]{0:T(256)(128)(2,1)} %dynamic-slice.43, ...), channel_id=1, replica_groups=mesh['dp'=8,'seq'=4] {'seq'}, use_global_device_ids=true, to_apply=%region_17.18 | all-reduce | flops 1152 | bytes 4608 | tf_op jit(solution)/shard_map/psum | solution.py:356
  1067.3 3.5 fusion.87
  1070.8 8.2 all-reduce.23.cloned.1.call-done
  (366 shorter events, 302.6 us)
Async XLA Ops:
  7.2 4.9 copy-start.31
  7.2 34.9 %copy-start.1 = (bf16[3,256,768]{2,1,0:T(8,128)(2,1)S(1)}, bf16[3,256,768]{2,1,0:T(8,128)(2,1)}, u32[]{:S(2)}) copy-start(bf16[3,256,768]{2,1,0:T(8,128)(2,1)} %param.22) | copy-start | bytes 3538948
  7.2 6.1 copy-start.36
  7.2 6.4 copy-start.37
  7.2 6.6 copy-start.38
  7.2 6.8 copy-start.39
  7.3 7.0 copy-start.40
  7.3 7.3 copy-start.41
  7.3 7.5 copy-start.42
  7.3 7.7 copy-start.43
  7.3 35.4 %all-gather.8.cloned.1.call-start = ((), (), s32[]{:S(2)}) async-start(), calls=%async_computation.14 | async-start | bytes 1327104 | tf_op jit(solution)/shard_map/all_gather | solution.py:142
  8.0 54.9 %all-gather.12.cloned.1.call-start = ((), (), s32[]{:S(2)}) async-start(), calls=%async_computation.16 | async-start | bytes 1327104 | tf_op jit(solution)/shard_map/all_gather | solution.py:145
  10.3 31.3 %copy-start.18 = (f32[3,256]{1,0:T(4,128)}, f32[3,256]{1,0:T(4,128)S(1)}, u32[]{:S(2)}) copy-start(f32[3,256]{1,0:T(4,128)S(1)} %broadcast_multiply_fusion.5) | copy-start | bytes 9220
  12.1 30.6 %copy-start.19 = (f32[768]{0:T(1024)}, f32[768]{0:T(1024)S(1)}, u32[]{:S(2)}) copy-start(f32[768]{0:T(1024)S(1)} %div.35) | copy-start | bytes 9220
  42.7 2.8 copy-start.9
  47.7 38.8 %all-to-all-start = ((bf16[3,256,768]{1,0,2:T(4,128)(2,1)}), bf16[3,256,768]{1,0,2:T(4,128)(2,1)S(1)}, u32[]{:S(2)}, u32[]{:S(2)}) async-start(bf16[3,256,768]{1,0,2:T(4,128)(2,1)} %copy.100), calls=%async_computation | async-start | bytes 3145728 | tf_op jit(solution)/shard_map/all_to_all | solution.py:170
  52.6 38.8 %all-gather.10.cloned.1.call-start = ((), (), s32[]{:S(2)}) async-start(), calls=%async_computation.15 | async-start | bytes 1327104 | tf_op jit(solution)/shard_map/all_gather | solution.py:144
  86.5 40.9 %all-to-all-start.2 = ((bf16[3,256,768]{1,0,2:T(4,128)(2,1)}), bf16[3,256,768]{1,0,2:T(4,128)(2,1)}, u32[]{:S(2)}, u32[]{:S(2)}) async-start(bf16[3,256,768]{1,0,2:T(4,128)(2,1)} %copy.106), calls=%async_computation.2 | async-start | bytes 3145728 | tf_op jit(solution)/shard_map/all_to_all | solution.py:184
  90.8 270.2 %all-gather.14.cloned.1.call-start = ((), (), s32[]{:S(2)}) async-start(), calls=%async_computation.17 | async-start | bytes 1327104 | tf_op jit(solution)/shard_map/all_gather | solution.py:147
  98.7 33.6 %copy-start.26 = (s32[3,256]{1,0:T(4,128)S(1)}, s32[3,256]{1,0:T(4,128)}, u32[]{:S(2)}) copy-start(s32[3,256]{1,0:T(4,128)} %param.23) | copy-start | bytes 9220
  127.3 63.0 %all-to-all-start.1 = ((bf16[3,256,768]{1,0,2:T(4,128)(2,1)}), bf16[3,256,768]{1,0,2:T(4,128)(2,1)}, u32[]{:S(2)}, u32[]{:S(2)}) async-start(bf16[3,256,768]{1,0,2:T(4,128)(2,1)} %copy.103), calls=%async_computation.1 | async-start | bytes 3145728 | tf_op jit(solution)/shard_map/all_to_all | solution.py:177
  131.7 232.6 %all-gather.16.cloned.1.call-start = ((), (), s32[]{:S(2)}) async-start(), calls=%async_computation.18 | async-start | bytes 5308416 | tf_op jit(solution)/shard_map/all_gather | solution.py:151
  204.5 1.9 copy-start
  215.5 1.9 copy-start
  226.6 1.9 copy-start
  237.6 1.9 copy-start
  248.6 1.9 copy-start
  259.6 1.9 copy-start
  270.6 1.9 copy-start
  281.7 1.9 copy-start
  292.7 1.9 copy-start
  301.3 4.3 copy-start.4
  305.5 5.2 copy-start.30
  305.5 5.2 copy-start.29
  305.5 5.2 copy-start.28
  305.5 50.2 %all-to-all-start.3 = ((bf16[3,1024,192]{2,0,1:T(4,128)(2,1)}), bf16[3,1024,192]{2,0,1:T(4,128)(2,1)}, u32[]{:S(2)}, u32[]{:S(2)}) async-start(bf16[3,1024,192]{2,0,1:T(4,128)(2,1)} %copy.112), calls=%async_computation.3 | async-start | bytes 4194304 | tf_op jit(solution)/shard_map/all_to_all | solution.py:201
  310.1 81.4 %all-gather.18.cloned.1.call-start = ((), (), s32[]{:S(2)}) async-start(), calls=%async_computation.19 | async-start | bytes 5308416 | tf_op jit(solution)/shard_map/all_gather | solution.py:153
  391.5 11.6 %copy-start.32 = (bf16[768,3072]{1,0:T(8,128)(2,1)S(1)}, bf16[768,3072]{1,0:T(8,128)(2,1)}, u32[]{:S(2)}) copy-start(bf16[768,3072]{1,0:T(8,128)(2,1)} %all-gather.16.cloned.1.call-done) | copy-start | bytes 14155780
  403.2 4.8 copy-start.8
  403.2 4.8 copy-start.7
  408.0 1.7 copy-start.35
  409.7 2.2 copy-start.5
  415.4 40.9 %all-to-all-start.4 = ((bf16[3,256,768]{1,0,2:T(4,128)(2,1)}), bf16[3,256,768]{1,0,2:T(4,128)(2,1)}, u32[]{:S(2)}, u32[]{:S(2)}) async-start(bf16[3,256,768]{1,0,2:T(4,128)(2,1)} %copy.115), calls=%async_computation.4 | async-start | bytes 3145728 | tf_op jit(solution)/shard_map/all_to_all | solution.py:252
  419.8 418.5 %reduce-scatter.13.cloned.1.call-start = ((), (), s32[]{:S(2)}) async-start(), calls=%async_computation.23 | async-start | bytes 2654208 | tf_op jit(solution)/shard_map/reduce_scatter | solution.py:330
  595.3 52.1 %all-to-all-start.5 = ((bf16[3,1024,192]{2,0,1:T(4,128)(2,1)}), bf16[3,1024,192]{2,0,1:T(4,128)(2,1)}, u32[]{:S(2)}, u32[]{:S(2)}) async-start(bf16[3,1024,192]{2,0,1:T(4,128)(2,1)} %copy.122), calls=%async_computation.5 | async-start | bytes 4194304 | tf_op jit(solution)/shard_map/all_to_all | solution.py:265
  599.8 244.3 %reduce-scatter.7.cloned.1.call-start = ((), (), s32[]{:S(2)}) async-start(), calls=%async_computation.20 | async-start | bytes 2654208 | tf_op jit(solution)/shard_map/reduce_scatter | solution.py:325
  659.9 185.7 %reduce-scatter.9.cloned.1.call-start = ((), (), s32[]{:S(2)}) async-start(), calls=%async_computation.21 | async-start | bytes 2654208 | tf_op jit(solution)/shard_map/reduce_scatter | solution.py:327
  726.4 120.9 %reduce-scatter.11.cloned.1.call-start = ((), (), s32[]{:S(2)}) async-start(), calls=%async_computation.22 | async-start | bytes 2654208 | tf_op jit(solution)/shard_map/reduce_scatter | solution.py:328
  781.3 1.4 copy-start.2
  793.5 123.4 %reduce-scatter.15.cloned.1.call-start = ((), (), s32[]{:S(2)}) async-start(), calls=%async_computation.24 | async-start | bytes 10616832 | tf_op jit(solution)/shard_map/reduce_scatter | solution.py:334
  802.5 194.2 %reduce-scatter.17.cloned.1.call-start = ((), (), s32[]{:S(2)}) async-start(), calls=%async_computation.25 | async-start | bytes 10616832 | tf_op jit(solution)/shard_map/reduce_scatter | solution.py:336
  813.2 1.6 copy-start.27
  813.2 265.8 %all-reduce.23.cloned.1.call-start = ((), (), s32[]{:S(2)}) async-start(), calls=%async_computation.26 | async-start | bytes 3538944 | tf_op jit(solution)/shard_map/psum | solution.py:358
  825.8 7.0 copy-start.3
  849.0 149.9 %copy-start.10 = (bf16[768,768]{1,0:T(8,128)(2,1)S(1)}, bf16[768,768]{1,0:T(8,128)(2,1)}, u32[]{:S(2)}) copy-start(bf16[768,768]{1,0:T(8,128)(2,1)} %reshape.310) | copy-start | bytes 3538948
  849.0 149.9 %copy-start.34 = (bf16[768,768]{1,0:T(8,128)(2,1)S(1)}, bf16[768,768]{1,0:T(8,128)(2,1)}, u32[]{:S(2)}) copy-start(bf16[768,768]{1,0:T(8,128)(2,1)} %all-gather.10.cloned.1.call-done) | copy-start | bytes 3538948
  999.0 1.6 copy-start.33
  999.0 2.4 copy-start.44
  1001.3 3.8 copy-start.25
  1001.3 65.9 %copy-start.6 = (f32[768,768]{1,0:T(8,128)S(1)}, f32[768,768]{1,0:T(8,128)}, u32[]{:S(2)}) copy-start(f32[768,768]{1,0:T(8,128)} %copy-done.5) | copy-start | bytes 7077892
  1079.0 4.4 copy-start.15
  1079.0 5.1 copy-start.14
  1079.0 5.9 copy-start.13
  1079.0 6.6 copy-start.12
  (8 other events, 9.0 us)
Sparse Core Ops, SparseCore 0:
  10.0 26.8 all-gather.7
  38.8 24.0 all-gather.11
  64.8 24.0 all-gather.9
  93.2 26.1 all-gather.13
  134.1 41.8 all-gather.15
  312.5 41.8 all-gather.17
  424.5 45.4 reduce-scatter.12
  660.0 43.1 reduce-scatter.6
  726.5 43.1 reduce-scatter.8
  793.6 43.2 reduce-scatter.10
  840.4 76.4 reduce-scatter.14
  920.2 76.4 reduce-scatter.16
  1000.7 78.2 all-reduce.22
where the time goes:
time: 1110 us; the launch traced here: 1090 us
  waiting for transfers between devices  323 us (29%)
  matrix products  266 us (24%)
  blocking collectives  219 us (20%)
  local copies, waits for them, and re-layouts  172 us (15%)
  other arithmetic  68 us (6%)
  starting transfers between devices  27.7 us (2%)
  between operations  16.7 us (2%)
    reduce_scatter x1, waiting for transfers between devices, per_device(): lax.psum_scatter(d_w_down, 'dp', scatter_dimension=0, tiled=True)  77.7 us
    reduce_scatter x1, waiting for transfers between devices, per_device(): lax.psum_scatter(d_w_up, 'dp', scatter_dimension=0, tiled=True)  67.9 us
    unnamed x2, blocking collectives  52.5 us
    all_to_all x1, blocking collectives, per_device(): lax.all_to_all(from_pairs(grad_key_pairs, seqs_here, heads_here), 'seq',...  51.4 us
    all_to_all x1, blocking collectives, per_device(): lax.all_to_all(from_pairs(grad_value_pairs, seqs_here, heads_here), 'seq'...  50.8 us
    all_to_all x1, waiting for transfers between devices, per_device(): lax.all_to_all(from_pairs(grad_query_pairs, seqs_here, heads_here), 'seq'...  45.4 us
    all_gather x1, blocking collectives, per_device(): full_segments = lax.all_gather(segment_ids, 'seq', axis=1, tiled=True)  41.2 us
    dot_general x18, matrix products, masked_scores(): jnp.einsum('qd,kd->qk', query_pair, key_pair, preferred_element_type=jnp....  38.3 us
  transfers between devices with their start and end apart: 19, of which 9 were waited for; matrix products, arithmetic and copies ran while one was open for 41% of the time, Pallas kernels for 0%

commit v1 on v0

--- a/solution.py
+++ b/solution.py
@@ -5,6 +5,29 @@
 
 HD = 64
 EPSILON = 1e-05
+
+
+def in_blocks(x, dim, length):
+    dims = x.shape
+    blocks = x.reshape(*dims[:dim], length, dims[dim] // length, *dims[dim + 1 :])
+    return jnp.moveaxis(blocks, dim, 0)
+
+
+def joined_along(blocks, dim):
+    shape = list(blocks.shape[1:])
+    shape[dim] *= blocks.shape[0]
+    return jnp.moveaxis(blocks, 0, dim).reshape(shape)
+
+
+def exchange_directly(x, axis, split_dim, concat_dim):
+    length, position = (lax.axis_size(axis), lax.axis_index(axis))
+    blocks = in_blocks(x, split_dim, length)
+    outs = [blocks[position]]
+    for turn in range(1, length):
+        sent = blocks[(position + turn) % length]
+        outs.append(lax.ppermute(sent, axis, [(i, (i + turn) % length) for i in range(length)]))
+    blocks = jnp.stack(outs)[(position - jnp.arange(length)) % length]
+    return joined_along(blocks, concat_dim)
 
 
 def layer_norm(values, gain, shift):
@@ -262,13 +285,7 @@
         ),
     )
     grad_query_tok, grad_key_tok, grad_value_tok = (
-        lax.all_to_all(
-            from_pairs(grad_query_pairs, seqs_here, heads_here),
-            "seq",
-            split_axis=1,
-            concat_axis=2,
-            tiled=True,
-        ),
+        exchange_directly(from_pairs(grad_query_pairs, seqs_here, heads_here), "seq", 1, 2),
         lax.all_to_all(
             from_pairs(grad_key_pairs, seqs_here, heads_here),
             "seq",

time: 1110 us -> 1090 us (0.982)
  waiting for transfers between devices: 323 us -> 299 us
    all_to_all x1 -> x0, waiting for transfers between devices: 45.4 us -> none  [per_device(): lax.all_to_all(from_pairs(grad_query_pairs, seqs_here, heads_here), 'seq'...]
    ppermute x0 -> x3, waiting for transfers between devices: none -> 16.4 us  [exchange_directly(): lax.ppermute(sent, axis, [(i, (i + turn) % length) for i in range(length)])]
    another operation x4 -> x7, local copies, waits for them, and re-layouts: 4.63 us -> 18 us
  transfers between devices with their start and end apart: 19 -> 21, of which waited for: 9 -> 10; matrix products, arithmetic and copies ran while one was open for 41% -> 42% of each run, Pallas kernels for 0% -> 0%
where the time goes in v1:
time: 1090 us; the launch traced here: 1080 us
  waiting for transfers between devices  299 us (27%)
  matrix products  266 us (24%)
  blocking collectives  223 us (20%)
  local copies, waits for them, and re-layouts  176 us (16%)
  other arithmetic  67.8 us (6%)
  starting transfers between devices  27.3 us (3%)
  between operations  16.8 us (2%)
    reduce_scatter x1, waiting for transfers between devices, per_device(): lax.psum_scatter(d_w_down, 'dp', scatter_dimension=0, tiled=True)  77.7 us
    reduce_scatter x1, waiting for transfers between devices, per_device(): lax.psum_scatter(d_w_up, 'dp', scatter_dimension=0, tiled=True)  74 us
    all_to_all x1, blocking collectives, per_device(): lax.all_to_all(from_pairs(grad_key_pairs, seqs_here, heads_here), 'seq',...  54.8 us
    unnamed x2, blocking collectives  52.5 us
    all_to_all x1, blocking collectives, per_device(): lax.all_to_all(from_pairs(grad_value_pairs, seqs_here, heads_here), 'seq'...  50.8 us
    all_gather x1, blocking collectives, per_device(): full_segments = lax.all_gather(segment_ids, 'seq', axis=1, tiled=True)  41.2 us
    dot_general x18, matrix products, masked_scores(): jnp.einsum('qd,kd->qk', query_pair, key_pair, preferred_element_type=jnp....  38.4 us
    dot_general x9, matrix products, attend_forward(): jnp.dot(probs, value_pair, preferred_element_type=jnp.float32)  37.7 us
  transfers between devices with their start and end apart: 21, of which 10 were waited for; matrix products, arithmetic and copies ran while one was open for 42% of the time, Pallas kernels for 0%

profile of v1, /device:TPU:0, one launch (start us, length us, event | category | flops | bytes accessed | tf_op | source)
XLA Modules:
  0.0 1076.5 jit_solution(9071887962067162375)
XLA Ops:
  15.2 26.3 %all-reduce.18 = (bf16[768]{0:T(1024)(128)(2,1)S(1)}, bf16[768]{0:T(1024)(128)(2,1)S(1)}, bf16[768]{0:T(1024)(128)(2,1)S(1)}, bf16[768]{0:T(1024)(128)(2,1)S(1)}...) all-reduce(bf16[768]{0:T(1024)(128)(2,1)S(1)} %dynamic-update-slice, ...), channel_id=1, replica_groups=mesh['dp'=8,'seq'=4] {'dp'}, use_global_device_ids=true, to_apply=%add.1 | all-reduce | flops 6144 | bytes 24576
  47.7 5.0 all-to-all-start
  53.4 9.6 all-gather.12.cloned.1.call-done
  62.9 3.7 add_convert_fusion.2
  66.7 3.6 copy.105
  70.3 16.2 %all-to-all-done = bf16[3,256,768]{1,0,2:T(4,128)(2,1)S(1)} async-done(((bf16[3,256,768]{1,0,2:T(4,128)(2,1)}), bf16[3,256,768]{1,0,2:T(4,128)(2,1)S(1)}, u32[]{:S(2)}, u32[]{:S(2)}) %all-to-all-start) | async-done | bytes 1179680 | tf_op jit(solution)/shard_map/all_to_all | solution.py:193
  86.5 4.4 all-to-all-start.2
  91.4 3.7 convolution_convert_fusion.1
  95.2 3.6 copy.102
  98.7 28.6 %all-to-all-done.2 = bf16[3,256,768]{1,0,2:T(4,128)(2,1)} async-done(((bf16[3,256,768]{1,0,2:T(4,128)(2,1)}), bf16[3,256,768]{1,0,2:T(4,128)(2,1)}, u32[]{:S(2)}, u32[]{:S(2)}) %all-to-all-start.2) | async-done | bytes 1179680 | tf_op jit(solution)/shard_map/all_to_all | solution.py:207
  127.3 4.3 all-to-all-start.1
  132.3 41.2 %all_gather.56 = s32[3,1024]{1,0:T(4,128)S(1)} all-gather(s32[3,256]{1,0:T(4,128)S(1)} %copy-done.31), channel_id=1, replica_groups=mesh['dp'=8,'seq'=4] {'seq'}, dimensions={1}, use_global_device_ids=true | all-gather | bytes 15360 | tf_op jit(solution)/shard_map/all_gather | solution.py:179
  183.2 3.4 reshape.344
  186.6 3.7 copy.110
  197.2 3.7 copy.109
  202.0 99.5 %while.26 = (s32[]{:T(128)}, bf16[9,1024,64]{1,2,0:T(8,128)(2,1)}, f32[9,1024]{1,0:T(8,128)}, s32[9,1024]{1,0:T(8,128)}, bf16[9,1024,64]{2,1,0:T(8,128)(2,1)S(1)...) while((s32[]{:T(128)}, bf16[9,1024,64]{1,2,0:T(8,128)(2,1)}, ...), condition=%wide.region_5.6_spmd, body=%wide.region_2.5_spmd.sunk | while | flops 284228608 | bytes 30349440 | solution.py:220
  208.9 4.2 fusion.158
  220.0 4.2 fusion.158
  231.0 4.2 fusion.158
  242.1 4.2 fusion.158
  253.1 4.2 fusion.158
  264.2 4.2 fusion.158
  275.2 4.2 fusion.158
  286.3 4.2 fusion.158
  297.3 4.2 fusion.158
  301.5 4.3 copy.111
  305.8 4.6 all-to-all-start.3
  311.7 10.1 all-gather
  322.4 33.6 %all-to-all-done.3 = bf16[3,1024,192]{2,0,1:T(4,128)(2,1)} async-done(((bf16[3,1024,192]{2,0,1:T(4,128)(2,1)}), bf16[3,1024,192]{2,0,1:T(4,128)(2,1)}, u32[]{:S(2)}, u32[]{:S(2)}) %all-to-all-start.3) | async-done | bytes 1179680 | tf_op jit(solution)/shard_map/all_to_all | solution.py:224
  364.5 27.3 %fusion.56 = (bf16[768,3072]{1,0:T(8,128)(2,1)}, f32[768,3072]{1,0:T(8,128)}) fusion(f32[3072]{0:T(1024)} %bitcast.299, bf16[768,3072]{1,0:T(8,128)(2,1)} %all-gather.16.cloned.1.call-done, f32[768,768]{1,0:T(8,128)S(1)} %get-tuple-element.269, f32[768]{0:T(1024)S(1)} %convert_element_type.227, f32[768]{0:T(1024)S(1)} %convert_element_type.226, ...), kind=kOutput, calls=%fused_computation.65 | convolution fusion | flops 3782541312 | bytes 21258240 | tf_op jit(solution)/shard_map/dot_general | solution.py:236
  391.8 11.6 %convert_reduce_fusion = (f32[3072]{0:T(1024)}, bf16[768,3072]{1,0:T(8,128)(2,1)S(1)}) fusion(f32[768,3072]{1,0:T(8,128)} %get-tuple-element.271, f32[3072]{0:T(1024)} %bitcast.300, bf16[768,768]{1,0:T(8,128)(2,1)} %bitcast.266, bf16[3072,768]{1,0:T(8,128)(2,1)} %all-gather.18.cloned.1.call-done), kind=kOutput, calls=%fused_computation.72 | convolution fusion | flops 3654546432 | bytes 20078592 | tf_op jit(solution)/shard_map/dot_general | solution.py:63
  403.4 4.8 multiply_reduce_fusion.1
  412.1 3.6 copy.114
  415.7 4.4 all-to-all-start.4
  420.7 4.6 fusion.92
  425.3 31.3 %all-to-all-done.4 = bf16[3,256,768]{1,0,2:T(4,128)(2,1)} async-done(((bf16[3,256,768]{1,0,2:T(4,128)(2,1)}), bf16[3,256,768]{1,0,2:T(4,128)(2,1)}, u32[]{:S(2)}, u32[]{:S(2)}) %all-to-all-start.4) | async-done | bytes 1179680 | tf_op jit(solution)/shard_map/all_to_all | solution.py:275
  460.1 3.8 reshape.352
  467.3 124.2 %while.27 = (s32[]{:T(128)}, bf16[9,1024,64]{1,2,0:T(8,128)(2,1)}, bf16[9,1024,64]{1,2,0:T(8,128)(2,1)}, bf16[9,1024,64]{1,2,0:T(8,128)(2,1)}, s32[9,1024]{1,0:T...) while((s32[]{:T(128)}, bf16[9,1024,64]{1,2,0:T(8,128)(2,1)}, ...), condition=%wide.region_12.13_spmd, body=%wide.region_10.12_spmd.sunk | while | flops 681901056 | bytes 33465460 | solution.py:276
  591.5 3.5 reshape_reshape.6
  595.0 5.9 constant_dynamic-slice_fusion.6
  607.3 5.6 collective-permute-done
  612.9 10.8 collective-permute-done.1
  627.8 3.6 copy.121
  631.4 4.0 reshape_reshape.7
  635.4 4.1 fusion.101
  639.6 4.3 copy.122
  643.9 54.8 %all_to_all.105 = bf16[3,1024,192]{2,0,1:T(4,128)(2,1)S(1)} all-to-all(bf16[3,1024,192]{2,0,1:T(4,128)(2,1)} %copy.122), channel_id=1, replica_groups=mesh['dp'=8,'seq'=4] {'seq'}, dimensions={1} | all-to-all | bytes 2359296 | tf_op jit(solution)/shard_map/all_to_all | solution.py:289
  701.4 4.0 reshape.357
  705.4 4.2 fusion.102
  709.7 4.1 copy.125
  713.7 50.8 %all_to_all.106 = bf16[3,1024,192]{2,0,1:T(4,128)(2,1)S(1)} all-to-all(bf16[3,1024,192]{2,0,1:T(4,128)(2,1)} %copy.125), channel_id=1, replica_groups=mesh['dp'=8,'seq'=4] {'seq'}, dimensions={1} | all-to-all | bytes 2359296 | tf_op jit(solution)/shard_map/all_to_all | solution.py:296
  768.6 4.0 reshape.360
  772.6 4.1 fusion.103
  776.8 9.0 fusion.95
  786.1 10.5 fusion.104
  800.3 8.7 add_convert_fusion
  809.9 4.3 fusion.99
  826.3 74.0 %reduce-scatter.15.cloned.1.call-done = f32[96,3072]{1,0:T(8,128)} async-done(((f32[768,3072]{1,0:T(8,128)}), f32[96,3072]{1,0:T(8,128)}) %reduce-scatter.15.cloned.1.call-update) | async-done | bytes 1179664 | tf_op jit(solution)/shard_map/reduce_scatter | solution.py:351
  902.4 77.7 %reduce-scatter.17.cloned.1.call-done = f32[384,768]{1,0:T(8,128)} async-done(((f32[3072,768]{1,0:T(8,128)}), f32[384,768]{1,0:T(8,128)}) %reduce-scatter.17.cloned.1.call-update) | async-done | bytes 1179664 | tf_op jit(solution)/shard_map/reduce_scatter | solution.py:353
  984.7 3.8 fusion.88
  988.5 26.3 %all-reduce.17 = (bf16[768]{0:T(1024)(128)(2,1)}, bf16[768]{0:T(1024)(128)(2,1)}, bf16[768]{0:T(1024)(128)(2,1)}, bf16[768]{0:T(1024)(128)(2,1)}, bf16[768]{0:T(...) all-reduce(f32[768]{0:T(1024)} %get-tuple-element.184, ...), channel_id=2, replica_groups=mesh['dp'=8,'seq'=4] {'dp'}, use_global_device_ids=true, to_apply=%region_16.17.clone | all-reduce | flops 9216 | bytes 55296
  1025.5 13.1 %all-reduce.19 = (bf16[96]{0:T(256)(128)(2,1)}, bf16[96]{0:T(256)(128)(2,1)}, bf16[96]{0:T(256)(128)(2,1)}, bf16[96]{0:T(256)(128)(2,1)}, bf16[96]{0:T(256)(128)...) all-reduce(bf16[96]{0:T(256)(128)(2,1)} %dynamic-slice.63, ...), channel_id=1, replica_groups=mesh['dp'=8,'seq'=4] {'seq'}, use_global_device_ids=true, to_apply=%region_17.18 | all-reduce | flops 1152 | bytes 4608 | tf_op jit(solution)/shard_map/psum | solution.py:373
  1050.5 3.5 fusion.87
  1054.0 8.4 all-reduce.23.cloned.1.call-done
  (389 shorter events, 309.8 us)
Async XLA Ops:
  7.2 4.9 copy-start.36
  7.2 34.9 %copy-start.1 = (bf16[3,256,768]{2,1,0:T(8,128)(2,1)S(1)}, bf16[3,256,768]{2,1,0:T(8,128)(2,1)}, u32[]{:S(2)}) copy-start(bf16[3,256,768]{2,1,0:T(8,128)(2,1)} %param.22) | copy-start | bytes 3538948
  7.2 6.1 copy-start.42
  7.2 6.4 copy-start.43
  7.2 6.6 copy-start.44
  7.2 6.8 copy-start.45
  7.3 7.0 copy-start.46
  7.3 7.3 copy-start.47
  7.3 7.5 copy-start.48
  7.3 7.7 copy-start.49
  7.3 35.4 %all-gather.8.cloned.1.call-start = ((), (), s32[]{:S(2)}) async-start(), calls=%async_computation.13 | async-start | bytes 1327104 | tf_op jit(solution)/shard_map/all_gather | solution.py:165
  8.0 54.9 %all-gather.12.cloned.1.call-start = ((), (), s32[]{:S(2)}) async-start(), calls=%async_computation.15 | async-start | bytes 1327104 | tf_op jit(solution)/shard_map/all_gather | solution.py:168
  10.3 31.3 %copy-start.20 = (f32[3,256]{1,0:T(4,128)}, f32[3,256]{1,0:T(4,128)S(1)}, u32[]{:S(2)}) copy-start(f32[3,256]{1,0:T(4,128)S(1)} %broadcast_multiply_fusion.5) | copy-start | bytes 9220
  12.1 30.6 %copy-start.22 = (f32[768]{0:T(1024)}, f32[768]{0:T(1024)S(1)}, u32[]{:S(2)}) copy-start(f32[768]{0:T(1024)S(1)} %div.35) | copy-start | bytes 9220
  42.7 2.8 copy-start.10
  47.7 38.8 %all-to-all-start = ((bf16[3,256,768]{1,0,2:T(4,128)(2,1)}), bf16[3,256,768]{1,0,2:T(4,128)(2,1)S(1)}, u32[]{:S(2)}, u32[]{:S(2)}) async-start(bf16[3,256,768]{1,0,2:T(4,128)(2,1)} %copy.99), calls=%async_computation | async-start | bytes 3145728 | tf_op jit(solution)/shard_map/all_to_all | solution.py:193
  52.6 38.8 %all-gather.10.cloned.1.call-start = ((), (), s32[]{:S(2)}) async-start(), calls=%async_computation.14 | async-start | bytes 1327104 | tf_op jit(solution)/shard_map/all_gather | solution.py:167
  86.5 40.9 %all-to-all-start.2 = ((bf16[3,256,768]{1,0,2:T(4,128)(2,1)}), bf16[3,256,768]{1,0,2:T(4,128)(2,1)}, u32[]{:S(2)}, u32[]{:S(2)}) async-start(bf16[3,256,768]{1,0,2:T(4,128)(2,1)} %copy.105), calls=%async_computation.2 | async-start | bytes 3145728 | tf_op jit(solution)/shard_map/all_to_all | solution.py:207
  90.8 270.4 %all-gather.14.cloned.1.call-start = ((), (), s32[]{:S(2)}) async-start(), calls=%async_computation.16 | async-start | bytes 1327104 | tf_op jit(solution)/shard_map/all_gather | solution.py:170
  98.7 33.6 %copy-start.31 = (s32[3,256]{1,0:T(4,128)S(1)}, s32[3,256]{1,0:T(4,128)}, u32[]{:S(2)}) copy-start(s32[3,256]{1,0:T(4,128)} %param.23) | copy-start | bytes 9220
  127.3 62.9 %all-to-all-start.1 = ((bf16[3,256,768]{1,0,2:T(4,128)(2,1)}), bf16[3,256,768]{1,0,2:T(4,128)(2,1)}, u32[]{:S(2)}, u32[]{:S(2)}) async-start(bf16[3,256,768]{1,0,2:T(4,128)(2,1)} %copy.102), calls=%async_computation.1 | async-start | bytes 3145728 | tf_op jit(solution)/shard_map/all_to_all | solution.py:200
  131.7 232.8 %all-gather.16.cloned.1.call-start = ((), (), s32[]{:S(2)}) async-start(), calls=%async_computation.17 | async-start | bytes 5308416 | tf_op jit(solution)/shard_map/all_gather | solution.py:174
  204.5 2.0 copy-start
  226.6 2.0 copy-start
  237.7 2.0 copy-start
  248.7 2.0 copy-start
  259.8 2.0 copy-start
  301.5 4.3 copy-start.5
  305.8 5.2 copy-start.35
  305.8 5.2 copy-start.34
  305.8 5.2 copy-start.33
  305.8 50.1 %all-to-all-start.3 = ((bf16[3,1024,192]{2,0,1:T(4,128)(2,1)}), bf16[3,1024,192]{2,0,1:T(4,128)(2,1)}, u32[]{:S(2)}, u32[]{:S(2)}) async-start(bf16[3,1024,192]{2,0,1:T(4,128)(2,1)} %copy.111), calls=%async_computation.3 | async-start | bytes 4194304 | tf_op jit(solution)/shard_map/all_to_all | solution.py:224
  310.4 81.4 %all-gather.18.cloned.1.call-start = ((), (), s32[]{:S(2)}) async-start(), calls=%async_computation.18 | async-start | bytes 5308416 | tf_op jit(solution)/shard_map/all_gather | solution.py:176
  391.8 11.6 %copy-start.38 = (bf16[768,3072]{1,0:T(8,128)(2,1)S(1)}, bf16[768,3072]{1,0:T(8,128)(2,1)}, u32[]{:S(2)}) copy-start(bf16[768,3072]{1,0:T(8,128)(2,1)} %all-gather.16.cloned.1.call-done) | copy-start | bytes 14155780
  403.4 4.8 copy-start.9
  403.4 4.8 copy-start.8
  409.9 2.2 copy-start.6
  415.7 40.9 %all-to-all-start.4 = ((bf16[3,256,768]{1,0,2:T(4,128)(2,1)}), bf16[3,256,768]{1,0,2:T(4,128)(2,1)}, u32[]{:S(2)}, u32[]{:S(2)}) async-start(bf16[3,256,768]{1,0,2:T(4,128)(2,1)} %copy.114), calls=%async_computation.4 | async-start | bytes 3145728 | tf_op jit(solution)/shard_map/all_to_all | solution.py:275
  420.1 399.7 %reduce-scatter.13.cloned.1.call-start = ((), (), s32[]{:S(2)}) async-start(), calls=%async_computation.22 | async-start | bytes 2654208 | tf_op jit(solution)/shard_map/reduce_scatter | solution.py:347
  425.3 396.1 %reduce-scatter.7.cloned.1.call-start = ((), (), s32[]{:S(2)}) async-start(), calls=%async_computation.19 | async-start | bytes 2654208 | tf_op jit(solution)/shard_map/reduce_scatter | solution.py:342
  600.9 4.2 copy-start.37
  600.9 4.8 copy-start.18
  600.9 4.8 copy-start.21
  600.9 4.8 copy-start.27
  600.9 4.8 copy-start.29
  601.0 11.9 %collective-permute-start = (bf16[3,256,192]{1,2,0:T(8,128)(2,1)S(1)}, bf16[3,256,192]{1,2,0:T(8,128)(2,1)S(1)}, u32[]{:S(2)}, u32[]{:S(2)}) collective-permute-start(bf16[3,256,192]{1,2,0:T(8,128)(2,1)S(1)} %bitcast.296), channel_id=1, source_target_pairs={{0,1},{1,2},{2,3},{3,0},{4,5},{5,6},{6,7},{7,4},{8,9},{9,10},{10,1... | collective-permute-start | bytes 884744 | tf_op jit(solution)/shard_map/ppermute | solution.py:28
  601.1 22.5 %collective-permute-start.1 = (bf16[3,256,192]{1,2,0:T(8,128)(2,1)S(1)}, bf16[3,256,192]{1,2,0:T(8,128)(2,1)S(1)}, u32[]{:S(2)}, u32[]{:S(2)}) collective-permute-start(bf16[3,256,192]{1,2,0:T(8,128)(2,1)S(1)} %bitcast.297), channel_id=1, source_target_pairs={{0,2},{1,3},{2,0},{3,1},{4,6},{5,7},{6,4},{7,5},{8,10},{9,11},{10,... | collective-permute-start | bytes 884744 | tf_op jit(solution)/shard_map/ppermute | solution.py:28
  603.2 20.4 %collective-permute-start.2 = (bf16[3,256,192]{1,2,0:T(8,128)(2,1)S(1)}, bf16[3,256,192]{1,2,0:T(8,128)(2,1)S(1)}, u32[]{:S(2)}, u32[]{:S(2)}) collective-permute-start(bf16[3,256,192]{1,2,0:T(8,128)(2,1)S(1)} %bitcast.298), channel_id=1, source_target_pairs={{0,3},{1,0},{2,1},{3,2},{4,7},{5,4},{6,5},{7,6},{8,11},{9,8},{10,9... | collective-permute-start | bytes 884744 | tf_op jit(solution)/shard_map/ppermute | solution.py:28
  639.6 183.4 %reduce-scatter.9.cloned.1.call-start = ((), (), s32[]{:S(2)}) async-start(), calls=%async_computation.20 | async-start | bytes 2654208 | tf_op jit(solution)/shard_map/reduce_scatter | solution.py:344
  709.6 115.0 %reduce-scatter.11.cloned.1.call-start = ((), (), s32[]{:S(2)}) async-start(), calls=%async_computation.21 | async-start | bytes 2654208 | tf_op jit(solution)/shard_map/reduce_scatter | solution.py:345
  776.8 123.5 %reduce-scatter.15.cloned.1.call-start = ((), (), s32[]{:S(2)}) async-start(), calls=%async_computation.23 | async-start | bytes 10616832 | tf_op jit(solution)/shard_map/reduce_scatter | solution.py:351
  785.8 194.3 %reduce-scatter.17.cloned.1.call-start = ((), (), s32[]{:S(2)}) async-start(), calls=%async_computation.24 | async-start | bytes 10616832 | tf_op jit(solution)/shard_map/reduce_scatter | solution.py:353
  796.6 265.7 %all-reduce.23.cloned.1.call-start = ((), (), s32[]{:S(2)}) async-start(), calls=%async_computation.25 | async-start | bytes 3538944 | tf_op jit(solution)/shard_map/psum | solution.py:375
  800.3 8.7 copy-start.4
  809.9 4.3 copy-start.3
  826.3 156.0 %copy-start.11 = (bf16[768,768]{1,0:T(8,128)(2,1)S(1)}, bf16[768,768]{1,0:T(8,128)(2,1)}, u32[]{:S(2)}) copy-start(bf16[768,768]{1,0:T(8,128)(2,1)} %reshape.357) | copy-start | bytes 3538948
  826.3 156.0 %copy-start.40 = (bf16[768,768]{1,0:T(8,128)(2,1)S(1)}, bf16[768,768]{1,0:T(8,128)(2,1)}, u32[]{:S(2)}) copy-start(bf16[768,768]{1,0:T(8,128)(2,1)} %all-gather.10.cloned.1.call-done) | copy-start | bytes 3538948
  982.3 2.4 copy-start.50
  984.7 3.8 copy-start.30
  984.7 65.8 %copy-start.7 = (f32[768,768]{1,0:T(8,128)S(1)}, f32[768,768]{1,0:T(8,128)}, u32[]{:S(2)}) copy-start(f32[768,768]{1,0:T(8,128)} %copy-done.6) | copy-start | bytes 7077892
  1062.3 4.4 copy-start.16
  1062.3 5.1 copy-start.15
  1062.4 5.9 copy-start.14
  1062.4 6.6 copy-start.13
  (16 other events, 22.9 us)
Sparse Core Ops, SparseCore 0:
  10.0 26.8 all-gather.7
  38.8 24.0 all-gather.11
  64.8 24.0 all-gather.9
  93.2 26.1 all-gather.13
  134.1 41.8 all-gather.15
  312.8 41.8 all-gather.17
  425.4 45.4 reduce-scatter.12
  639.7 47.7 reduce-scatter.6
  709.7 43.3 reduce-scatter.8
  776.9 43.2 reduce-scatter.10
  823.7 76.4 reduce-scatter.14
  903.6 76.4 reduce-scatter.16
  984.1 78.1 all-reduce.22
